TPU v7x, 32 devices: a whole 2x2x4 slice. The times are simulated.
32 devices in a mesh: seq: 8 (over z, x), head: 4 (over y, core).
Axes of the slice: x: 2, y: 2, z: 4, core: 2. Of those that a mesh axis runs over, the one named last changes fastest.
Arguments:
- query: bfloat16 [8192, 4096], P('seq', 'head'), may hold values from -140 to 140
- key: bfloat16 [8192, 512], P('seq'), may hold values from -7 to 7
- value: bfloat16 [8192, 512], P('seq'), may hold values from -6 to 6
- out_grad: bfloat16 [8192, 4096], P('seq', 'head'), may hold values from -6 to 6
- chosen: int32 [32, 16, 4], P('head', 'seq'), may hold values from 0 to 15, as said below
- drop_seed: int32 [32], P('head'), may hold values from 0 to 16777215
Outputs:
- query_grad: float32 [8192, 4096], P('seq', 'head')
- key_grad: float32 [8192, 512], P(('seq', 'head'))
- value_grad: float32 [8192, 512], P(('seq', 'head'))
Inputs may be any that keep to these rules, and one draw needn't show every extreme that they name: `chosen`: for head h and query block b, entry 0 is b; the other entries are distinct blocks before b whose shard lies at most 3 shards of 1024 tokens before the shard of b, or b itself where fewer such blocks exist.
All inputs are finite; a program needn't handle non-finite values.
Results may differ from a plain program's by a relative error of at most 0.014.
Values may be sent and summed in bfloat16 or wider, within the bound.
A program may use at most 128 MiB of HBM per device.

v0:
```python
import jax
import jax.numpy as jnp
from jax import lax
from jax.sharding import PartitionSpec as P

HD = 128
HEADS = 32
KVH = 4
BLK = 512
TOPK = 4
SPAN = 8


drop_cut = 6554
keep_gain = 1.0 / 0.9


def shifted(array, axis, by):
    size = lax.axis_size(axis)
    pairs = [(i, i + by) for i in range(size) if 0 <= i + by < size]
    return lax.ppermute(array, axis, pairs)


def keep_scale(seed_value, query_pos, key_pos):
    mixed = seed_value + query_pos[:, None] * 40503 + key_pos[None, :] * 9973
    mixed = mixed ^ jnp.right_shift(mixed, 15) & 131071
    mixed = mixed * 73244475
    mixed = mixed ^ jnp.right_shift(mixed, 13) & 524287
    return jnp.where(mixed & 65535 >= drop_cut, keep_gain, 0.0).astype(jnp.float32)


def block_grads(
    query_block, out_block, key_sel, value_sel, query_pos, key_pos, allowed, seed_value
):
    factor = key_sel.shape[-1] ** (-0.5)
    scores = jnp.dot(query_block, key_sel.T, preferred_element_type=jnp.float32) * factor
    scores = jnp.where(allowed, scores, -jnp.inf)
    peak = jnp.max(scores, axis=1, keepdims=True)
    total = jnp.sum(jnp.exp(scores - peak), axis=1, keepdims=True)
    probs = jnp.exp(scores - (peak + jnp.log(total)))
    gains = keep_scale(seed_value, query_pos, key_pos)
    dropped = (probs * gains).astype(jnp.bfloat16)
    output = jnp.dot(dropped, value_sel, preferred_element_type=jnp.float32)
    delta = jnp.sum(out_block.astype(jnp.float32) * output, axis=1, keepdims=True)
    pgrad = jnp.dot(out_block, value_sel.T, preferred_element_type=jnp.float32)
    sgrad = (probs * (pgrad * gains - delta)).astype(jnp.bfloat16)
    qgrad = jnp.dot(sgrad, key_sel, preferred_element_type=jnp.float32) * factor
    kgrad = jnp.dot(sgrad.T, query_block, preferred_element_type=jnp.float32) * factor
    vgrad = jnp.dot(dropped.T, out_block, preferred_element_type=jnp.float32)
    return (qgrad, kgrad, vgrad)


def local(query, key, value, out_grad, chosen, drop_seed):
    rows = query.shape[0]
    local_heads = query.shape[1] // HD
    local_blocks = rows // BLK
    window = min(SPAN, lax.axis_size("seq") // 2)
    shard = lax.axis_index("seq")
    head_rank = lax.axis_index("head")
    kv_col = head_rank * local_heads // (HEADS // KVH) * HD
    own_pair = jnp.stack(
        [
            lax.dynamic_slice_in_dim(key, kv_col, HD, 1),
            lax.dynamic_slice_in_dim(value, kv_col, HD, 1),
        ]
    )
    slots = [own_pair]
    moving = own_pair
    for offset in range(1, window):
        moving = shifted(moving, "seq", 1)
        slots.append(moving)
    stacked = jnp.stack(slots)
    offsets = jnp.arange(BLK, dtype=jnp.int32)

    def visit(index, carry):
        query_grad, partial_value = carry
        head = index // local_blocks
        block = index % local_blocks
        picks = lax.dynamic_index_in_dim(
            lax.dynamic_index_in_dim(chosen, head, 0, False), block, 0, False
        )
        seed_value = lax.dynamic_index_in_dim(drop_seed, head, 0, False)
        query_rows = block * BLK
        query_block = lax.dynamic_slice(query, (query_rows, head * HD), (BLK, HD))
        out_block = lax.dynamic_slice(out_grad, (query_rows, head * HD), (BLK, HD))
        places, key_parts, value_parts, pos_parts, live_parts = ([], [], [], [], [])
        for entry in range(TOPK):
            target = picks[entry]
            slot_index = shard - target // local_blocks
            within = target % local_blocks * BLK
            places.append((slot_index, within))
            pair = lax.dynamic_slice(stacked, (slot_index, 0, within, 0), (1, 2, BLK, HD))[0]
            key_parts.append(pair[0])
            value_parts.append(pair[1])
            pos_parts.append(target * BLK + offsets)
            if entry == 0:
                fresh = jnp.ones((BLK,), dtype=bool)
            else:
                fresh = jnp.broadcast_to(jnp.logical_not(jnp.any(picks[:entry] == target)), (BLK,))
            live_parts.append(fresh)
        key_pos = jnp.concatenate(pos_parts)
        query_pos = (shard * local_blocks + block) * BLK + offsets
        allowed = (key_pos[None, :] <= query_pos[:, None]) & jnp.concatenate(live_parts)[None, :]
        qgrad, kgrad, vgrad = block_grads(
            query_block,
            out_block,
            jnp.concatenate(key_parts),
            jnp.concatenate(value_parts),
            query_pos,
            key_pos,
            allowed,
            seed_value,
        )
        for entry in range(TOPK):
            slot_index, within = places[entry]
            update = jnp.stack(
                [kgrad[entry * BLK : (entry + 1) * BLK], vgrad[entry * BLK : (entry + 1) * BLK]]
            )[None]
            current = lax.dynamic_slice(partial_value, (slot_index, 0, within, 0), (1, 2, BLK, HD))
            partial_value = lax.dynamic_update_slice(
                partial_value, current + update, (slot_index, 0, within, 0)
            )
        query_grad = lax.dynamic_update_slice(query_grad, qgrad, (query_rows, head * HD))
        return (query_grad, partial_value)

    start_grad = jnp.zeros((rows, local_heads * HD), jnp.float32)
    start_partial = jnp.zeros((window, 2, rows, HD), jnp.float32)
    query_grad, partial_value = lax.fori_loop(
        0, local_heads * local_blocks, visit, (start_grad, start_partial)
    )
    carried = partial_value[window - 1]
    for offset in range(window - 1, 0, -1):
        carried = shifted(carried, "seq", -1) + partial_value[offset - 1]
    widened = lax.dynamic_update_slice(
        jnp.zeros((2, rows, KVH * HD), jnp.float32), carried, (0, 0, kv_col)
    )
    key_grad, value_grad = (
        lax.psum_scatter(widened[0], "head", scatter_dimension=0, tiled=True),
        lax.psum_scatter(widened[1], "head", scatter_dimension=0, tiled=True),
    )
    return (query_grad, key_grad, value_grad)


def solution(mesh):
    in_specs = (
        P("seq", "head"),
        P("seq", None),
        P("seq", None),
        P("seq", "head"),
        P("head", "seq", None),
        P("head"),
    )
    out_specs = (P("seq", "head"), P(("seq", "head"), None), P(("seq", "head"), None))
    return jax.shard_map(local, mesh=mesh, in_specs=in_specs, out_specs=out_specs, check_vma=False)
```

profile of v0, /device:TPU:8, one launch (start us, length us, event | category | flops | bytes accessed | tf_op | source)
XLA Modules:
  0.0 907.5 jit_solution(13377472558501188891)
XLA Ops:
  11.8 13.0 %collective-permute-done = bf16[2,1024,128]{2,1,0:T(8,128)(2,1)S(1)} collective-permute-done((bf16[2,1024,128]{2,1,0:T(8,128)(2,1)S(1)}, bf16[2,1024,128]{2,1,0:T(8,128)(2,1)S(1)}, u32[]{:S(2)}, u32[]{:S(2)}) %collective-permute-start) | collective-permute-done | bytes 524320 | tf_op jit(solution)/shard_map/ppermute | solution.py:21
  27.3 13.1 %collective-permute-done.1 = bf16[2,1024,128]{2,1,0:T(8,128)(2,1)S(1)} collective-permute-done((bf16[2,1024,128]{2,1,0:T(8,128)(2,1)S(1)}, bf16[2,1024,128]{2,1,0:T(8,128)(2,1)S(1)}, u32[]{:S(2)}, u32[]{:S(2)}) %collective-permute-start.1) | collective-permute-done | bytes 524320 | tf_op jit(solution)/shard_map/ppermute | solution.py:21
  42.4 12.8 %collective-permute-done.2 = bf16[2,1024,128]{2,1,0:T(8,128)(2,1)S(1)} collective-permute-done((bf16[2,1024,128]{2,1,0:T(8,128)(2,1)S(1)}, bf16[2,1024,128]{2,1,0:T(8,128)(2,1)S(1)}, u32[]{:S(2)}, u32[]{:S(2)}) %collective-permute-start.2) | collective-permute-done | bytes 524320 | tf_op jit(solution)/shard_map/ppermute | solution.py:21
  62.3 691.4 %while.20 = (s32[]{:T(128)}, f32[1024,1024]{1,0:T(8,128)}, f32[4,2,1024,128]{3,2,1,0:T(8,128)}, s32[8,2,4]{0,2,1:T(4,128)S(1)}, s32[]{:T(128)}, /*index=5*/bf16[...) while((s32[]{:T(128)}, f32[1024,1024]{1,0:T(8,128)}, ...), condition=%wide.region_6.7_spmd.clone.clone, body=%wide.region_0.6_spmd.clone.clone.sunk | while | flops 1659388544 | bytes 81231872 | solution.py:128
  89.7 4.1 fusion.72
  132.9 4.1 fusion.72
  176.1 4.1 fusion.72
  219.3 4.1 fusion.72
  262.5 4.1 fusion.72
  305.7 4.1 fusion.72
  349.0 4.1 fusion.72
  392.2 4.1 fusion.72
  435.4 4.1 fusion.72
  478.6 4.1 fusion.72
  521.8 4.1 fusion.72
  608.2 4.1 fusion.72
  651.4 4.1 fusion.72
  737.8 4.1 fusion.72
  756.9 22.3 %collective-permute-done.3 = f32[2,1024,128]{2,1,0:T(8,128)S(1)} collective-permute-done((f32[2,1024,128]{2,1,0:T(8,128)S(1)}, f32[2,1024,128]{2,1,0:T(8,128)S(1)}, u32[]{:S(2)}, u32[]{:S(2)}) %collective-permute-start.3) | collective-permute-done | bytes 1048608 | tf_op jit(solution)/shard_map/ppermute | solution.py:21
  783.6 20.2 %collective-permute-done.4 = f32[2,1024,128]{2,1,0:T(8,128)S(1)} collective-permute-done((f32[2,1024,128]{2,1,0:T(8,128)S(1)}, f32[2,1024,128]{2,1,0:T(8,128)S(1)}, u32[]{:S(2)}, u32[]{:S(2)}) %collective-permute-start.4) | collective-permute-done | bytes 1048608 | tf_op jit(solution)/shard_map/ppermute | solution.py:21
  805.2 4.3 collective-permute-start.5
  809.5 19.2 %collective-permute-done.5 = f32[2,1024,128]{2,1,0:T(8,128)S(1)} collective-permute-done((f32[2,1024,128]{2,1,0:T(8,128)S(1)}, f32[2,1024,128]{2,1,0:T(8,128)S(1)}, u32[]{:S(2)}, u32[]{:S(2)}) %collective-permute-start.5) | collective-permute-done | bytes 1048608 | tf_op jit(solution)/shard_map/ppermute | solution.py:21
  833.8 32.6 %reduce-scatter.3.cloned.1.call-done = f32[256,512]{1,0:T(8,128)} async-done(((f32[1024,512]{1,0:T(8,128)}), f32[256,512]{1,0:T(8,128)}) %reduce-scatter.3.cloned.1.call-update) | async-done | bytes 524304 | tf_op jit(solution)/shard_map/reduce_scatter | solution.py:138
  866.4 34.3 %reduce-scatter.5.cloned.1.call-done = f32[256,512]{1,0:T(8,128)} async-done(((f32[1024,512]{1,0:T(8,128)}), f32[256,512]{1,0:T(8,128)}) %reduce-scatter.5.cloned.1.call-update) | async-done | bytes 524304 | tf_op jit(solution)/shard_map/reduce_scatter | solution.py:139
  (622 shorter events, 411.8 us)
Async XLA Ops:
  7.2 859.2 %reduce-scatter.3.cloned.1.call-start = ((), (), s32[]{:S(2)}) async-start(), calls=%async_computation.2 | async-start | bytes 2621440 | tf_op jit(solution)/shard_map/reduce_scatter | solution.py:138
  8.4 16.5 %collective-permute-start = (bf16[2,1024,128]{2,1,0:T(8,128)(2,1)S(1)}, bf16[2,1024,128]{2,1,0:T(8,128)(2,1)S(1)}, u32[]{:S(2)}, u32[]{:S(2)}) collective-permute-start(bf16[2,1024,128]{2,1,0:T(8,128)(2,1)S(1)} %get-tuple-element.426), channel_id=1, source_target_pairs={{0,4},{4,8},{8,12},{12,16},{16,20},{20,24},{24,28},{1,5},{5,9},{9,... | collective-permute-start | bytes 1572872 | tf_op jit(solution)/shard_map/ppermute | solution.py:21
  24.8 15.6 %collective-permute-start.1 = (bf16[2,1024,128]{2,1,0:T(8,128)(2,1)S(1)}, bf16[2,1024,128]{2,1,0:T(8,128)(2,1)S(1)}, u32[]{:S(2)}, u32[]{:S(2)}) collective-permute-start(bf16[2,1024,128]{2,1,0:T(8,128)(2,1)S(1)} %collective-permute-done), channel_id=1, source_target_pairs={{0,4},{4,8},{8,12},{12,16},{16,20},{20,24},{24,28},{1,5},{5,9},{9,... | collective-permute-start | bytes 1572872 | tf_op jit(solution)/shard_map/ppermute | solution.py:21
  40.4 14.7 %collective-permute-start.2 = (bf16[2,1024,128]{2,1,0:T(8,128)(2,1)S(1)}, bf16[2,1024,128]{2,1,0:T(8,128)(2,1)S(1)}, u32[]{:S(2)}, u32[]{:S(2)}) collective-permute-start(bf16[2,1024,128]{2,1,0:T(8,128)(2,1)S(1)} %collective-permute-done.1), channel_id=1, source_target_pairs={{0,4},{4,8},{8,12},{12,16},{16,20},{20,24},{24,28},{1,5},{5,9},{9,... | collective-permute-start | bytes 1572872 | tf_op jit(solution)/shard_map/ppermute | solution.py:21
  62.3 22.5 %copy-start.1 = (bf16[4,2,1024,128]{3,2,1,0:T(8,128)(2,1)}, bf16[4,2,1024,128]{3,2,1,0:T(8,128)(2,1)S(1)}, u32[]{:S(2)}) copy-start(bf16[4,2,1024,128]{3,2,1,0:T(8,128)(2,1)S(1)} %get-tuple-element.601) | copy-start | bytes 6291460 | tf_op jit(solution)/shard_map/while
  105.5 22.5 %copy-start.1 = (bf16[4,2,1024,128]{3,2,1,0:T(8,128)(2,1)}, bf16[4,2,1024,128]{3,2,1,0:T(8,128)(2,1)S(1)}, u32[]{:S(2)}) copy-start(bf16[4,2,1024,128]{3,2,1,0:T(8,128)(2,1)S(1)} %get-tuple-element.601) | copy-start | bytes 6291460 | tf_op jit(solution)/shard_map/while
  148.8 22.5 %copy-start.1 = (bf16[4,2,1024,128]{3,2,1,0:T(8,128)(2,1)}, bf16[4,2,1024,128]{3,2,1,0:T(8,128)(2,1)S(1)}, u32[]{:S(2)}) copy-start(bf16[4,2,1024,128]{3,2,1,0:T(8,128)(2,1)S(1)} %get-tuple-element.601) | copy-start | bytes 6291460 | tf_op jit(solution)/shard_map/while
  192.0 22.5 %copy-start.1 = (bf16[4,2,1024,128]{3,2,1,0:T(8,128)(2,1)}, bf16[4,2,1024,128]{3,2,1,0:T(8,128)(2,1)S(1)}, u32[]{:S(2)}) copy-start(bf16[4,2,1024,128]{3,2,1,0:T(8,128)(2,1)S(1)} %get-tuple-element.601) | copy-start | bytes 6291460 | tf_op jit(solution)/shard_map/while
  235.2 22.5 %copy-start.1 = (bf16[4,2,1024,128]{3,2,1,0:T(8,128)(2,1)}, bf16[4,2,1024,128]{3,2,1,0:T(8,128)(2,1)S(1)}, u32[]{:S(2)}) copy-start(bf16[4,2,1024,128]{3,2,1,0:T(8,128)(2,1)S(1)} %get-tuple-element.601) | copy-start | bytes 6291460 | tf_op jit(solution)/shard_map/while
  278.4 22.5 %copy-start.1 = (bf16[4,2,1024,128]{3,2,1,0:T(8,128)(2,1)}, bf16[4,2,1024,128]{3,2,1,0:T(8,128)(2,1)S(1)}, u32[]{:S(2)}) copy-start(bf16[4,2,1024,128]{3,2,1,0:T(8,128)(2,1)S(1)} %get-tuple-element.601) | copy-start | bytes 6291460 | tf_op jit(solution)/shard_map/while
  321.6 22.5 %copy-start.1 = (bf16[4,2,1024,128]{3,2,1,0:T(8,128)(2,1)}, bf16[4,2,1024,128]{3,2,1,0:T(8,128)(2,1)S(1)}, u32[]{:S(2)}) copy-start(bf16[4,2,1024,128]{3,2,1,0:T(8,128)(2,1)S(1)} %get-tuple-element.601) | copy-start | bytes 6291460 | tf_op jit(solution)/shard_map/while
  364.8 22.5 %copy-start.1 = (bf16[4,2,1024,128]{3,2,1,0:T(8,128)(2,1)}, bf16[4,2,1024,128]{3,2,1,0:T(8,128)(2,1)S(1)}, u32[]{:S(2)}) copy-start(bf16[4,2,1024,128]{3,2,1,0:T(8,128)(2,1)S(1)} %get-tuple-element.601) | copy-start | bytes 6291460 | tf_op jit(solution)/shard_map/while
  408.0 22.5 %copy-start.1 = (bf16[4,2,1024,128]{3,2,1,0:T(8,128)(2,1)}, bf16[4,2,1024,128]{3,2,1,0:T(8,128)(2,1)S(1)}, u32[]{:S(2)}) copy-start(bf16[4,2,1024,128]{3,2,1,0:T(8,128)(2,1)S(1)} %get-tuple-element.601) | copy-start | bytes 6291460 | tf_op jit(solution)/shard_map/while
  451.2 22.5 %copy-start.1 = (bf16[4,2,1024,128]{3,2,1,0:T(8,128)(2,1)}, bf16[4,2,1024,128]{3,2,1,0:T(8,128)(2,1)S(1)}, u32[]{:S(2)}) copy-start(bf16[4,2,1024,128]{3,2,1,0:T(8,128)(2,1)S(1)} %get-tuple-element.601) | copy-start | bytes 6291460 | tf_op jit(solution)/shard_map/while
  494.5 22.5 %copy-start.1 = (bf16[4,2,1024,128]{3,2,1,0:T(8,128)(2,1)}, bf16[4,2,1024,128]{3,2,1,0:T(8,128)(2,1)S(1)}, u32[]{:S(2)}) copy-start(bf16[4,2,1024,128]{3,2,1,0:T(8,128)(2,1)S(1)} %get-tuple-element.601) | copy-start | bytes 6291460 | tf_op jit(solution)/shard_map/while
  537.7 22.5 %copy-start.1 = (bf16[4,2,1024,128]{3,2,1,0:T(8,128)(2,1)}, bf16[4,2,1024,128]{3,2,1,0:T(8,128)(2,1)S(1)}, u32[]{:S(2)}) copy-start(bf16[4,2,1024,128]{3,2,1,0:T(8,128)(2,1)S(1)} %get-tuple-element.601) | copy-start | bytes 6291460 | tf_op jit(solution)/shard_map/while
  580.9 22.5 %copy-start.1 = (bf16[4,2,1024,128]{3,2,1,0:T(8,128)(2,1)}, bf16[4,2,1024,128]{3,2,1,0:T(8,128)(2,1)S(1)}, u32[]{:S(2)}) copy-start(bf16[4,2,1024,128]{3,2,1,0:T(8,128)(2,1)S(1)} %get-tuple-element.601) | copy-start | bytes 6291460 | tf_op jit(solution)/shard_map/while
  624.1 22.5 %copy-start.1 = (bf16[4,2,1024,128]{3,2,1,0:T(8,128)(2,1)}, bf16[4,2,1024,128]{3,2,1,0:T(8,128)(2,1)S(1)}, u32[]{:S(2)}) copy-start(bf16[4,2,1024,128]{3,2,1,0:T(8,128)(2,1)S(1)} %get-tuple-element.601) | copy-start | bytes 6291460 | tf_op jit(solution)/shard_map/while
  667.3 22.5 %copy-start.1 = (bf16[4,2,1024,128]{3,2,1,0:T(8,128)(2,1)}, bf16[4,2,1024,128]{3,2,1,0:T(8,128)(2,1)S(1)}, u32[]{:S(2)}) copy-start(bf16[4,2,1024,128]{3,2,1,0:T(8,128)(2,1)S(1)} %get-tuple-element.601) | copy-start | bytes 6291460 | tf_op jit(solution)/shard_map/while
  710.5 22.5 %copy-start.1 = (bf16[4,2,1024,128]{3,2,1,0:T(8,128)(2,1)}, bf16[4,2,1024,128]{3,2,1,0:T(8,128)(2,1)S(1)}, u32[]{:S(2)}) copy-start(bf16[4,2,1024,128]{3,2,1,0:T(8,128)(2,1)S(1)} %get-tuple-element.601) | copy-start | bytes 6291460 | tf_op jit(solution)/shard_map/while
  755.0 24.2 %collective-permute-start.3 = (f32[2,1024,128]{2,1,0:T(8,128)S(1)}, f32[2,1024,128]{2,1,0:T(8,128)S(1)}, u32[]{:S(2)}, u32[]{:S(2)}) collective-permute-start(f32[2,1024,128]{2,1,0:T(8,128)S(1)} %slice_bitcast_fusion.10), channel_id=1, source_target_pairs={{4,0},{8,4},{12,8},{16,12},{20,16},{24,20},{28,24},{5,1},{9,5},{13... | collective-permute-start | bytes 3145736 | tf_op jit(solution)/shard_map/ppermute | solution.py:21
  780.5 23.3 %collective-permute-start.4 = (f32[2,1024,128]{2,1,0:T(8,128)S(1)}, f32[2,1024,128]{2,1,0:T(8,128)S(1)}, u32[]{:S(2)}, u32[]{:S(2)}) collective-permute-start(f32[2,1024,128]{2,1,0:T(8,128)S(1)} %bitcast_add_fusion.2), channel_id=1, source_target_pairs={{4,0},{8,4},{12,8},{16,12},{20,16},{24,20},{28,24},{5,1},{9,5},{13... | collective-permute-start | bytes 3145736 | tf_op jit(solution)/shard_map/ppermute | solution.py:21
  805.2 23.5 %collective-permute-start.5 = (f32[2,1024,128]{2,1,0:T(8,128)S(1)}, f32[2,1024,128]{2,1,0:T(8,128)S(1)}, u32[]{:S(2)}, u32[]{:S(2)}) collective-permute-start(f32[2,1024,128]{2,1,0:T(8,128)S(1)} %bitcast_add_fusion.1), channel_id=1, source_target_pairs={{4,0},{8,4},{12,8},{16,12},{20,16},{24,20},{28,24},{5,1},{9,5},{13... | collective-permute-start | bytes 3145736 | tf_op jit(solution)/shard_map/ppermute | solution.py:21
  833.0 67.7 %reduce-scatter.5.cloned.1.call-start = ((), (), s32[]{:S(2)}) async-start(), calls=%async_computation.3 | async-start | bytes 2621440 | tf_op jit(solution)/shard_map/reduce_scatter | solution.py:139
  (36 other events, 188.9 us)
Sparse Core Ops, SparseCore 0:
  833.2 33.2 reduce-scatter.2
  869.5 31.1 reduce-scatter.4
where the time goes:
time: 917 us; the launch traced here: 908 us
  loops' own time  252 us (27%)
  other arithmetic  228 us (25%)
  matrix products  175 us (19%)
  waiting for transfers between devices  168 us (18%)
  local copies, waits for them, and re-layouts  53.8 us (6%)
  starting transfers between devices  17.2 us (2%)
  between operations  14.2 us (2%)
    another operation x1, loops' own time, local(): lax.fori_loop(0, local_heads * local_blocks, visit, (start_grad, start_pa...  252 us
    dynamic_update_slice x64, other arithmetic, visit(): lax.dynamic_update_slice(partial_value, current + update, (slot_index, 0,...  124 us
    ppermute x6, waiting for transfers between devices, shifted(): return lax.ppermute(array, axis, pairs)  101 us
    dot_general x16, matrix products, block_grads(): pgrad = jnp.dot(out_block, value_sel.T, preferred_element_type=jnp.float32)  66 us
    reduce_or x32, other arithmetic, visit(): jnp.any(picks[:entry] == target)  39.8 us
    convert_element_type x16, other arithmetic, block_grads(): dropped = (probs * gains).astype(jnp.bfloat16)  35.7 us
    reduce_scatter x1, waiting for transfers between devices, local(): lax.psum_scatter(widened[1], 'head', scatter_dimension=0, tiled=True)  34.3 us
    dot_general x16, matrix products, block_grads(): jnp.dot(query_block, key_sel.T, preferred_element_type=jnp.float32) * factor  34.1 us
  transfers between devices with their start and end apart: 8, of which 8 were waited for; matrix products, arithmetic and copies ran while one was open for 0% of the time, Pallas kernels for 0%

commit v1 on v0

v1 whole, which is shorter than its diff:
```python
import math

import jax
import jax.numpy as jnp
from jax import lax
from jax.experimental import pallas as pl
from jax.experimental.pallas import tpu as pltpu
from jax.sharding import PartitionSpec as P

HD = 128
HEADS = 32
KVH = 4
BLK = 512
TOPK = 4
SPAN = 8
SUB = 128

drop_cut = 6554
keep_gain = 1.0 / 0.9
factor = HD ** (-0.5)
exp_scale = factor * math.log2(math.e)


def shifted(array, axis, by):
    size = lax.axis_size(axis)
    pairs = [(i, i + by) for i in range(size) if 0 <= i + by < size]
    return lax.ppermute(array, axis, pairs)


def kept(x):
    x = x ^ lax.shift_right_logical(x, 15)
    x = x * 73244475
    x = x ^ lax.shift_right_logical(x, 13)
    return (x & 65535) >= drop_cut


def dot(a, b):
    return jnp.dot(a, b, preferred_element_type=jnp.float32)


def grads_kernel(local_blocks, window, steps, chosen_ref, seed_ref, shard_ref, q_ref, do_ref, kv_ref,
                 qg_ref, far_ref, own_ref, s_ref, pg_ref, d_ref, sg_ref, acc_ref, kt_ref, hash_ref):
    step = pl.program_id(0)

    @pl.when(step == 0)
    def _():
        acc_ref[...] = jnp.zeros_like(acc_ref)
        d_ref[0] = jnp.zeros((BLK, BLK), jnp.bfloat16)
        sg_ref[0] = jnp.zeros((BLK, BLK), jnp.bfloat16)
        for slot in range(window):
            kt_ref[slot] = kv_ref[slot, 0].T
        hash_ref[...] = (lax.broadcasted_iota(jnp.int32, (BLK, BLK), 0) * 9973
                         + lax.broadcasted_iota(jnp.int32, (BLK, BLK), 1) * 40503)

    head = step // local_blocks
    block = lax.rem(step, local_blocks)
    shard = shard_ref[0]
    own_block = shard * local_blocks + block
    picks = [chosen_ref[step * TOPK + t] for t in range(TOPK)]
    places = []
    live = [None]
    for t in range(TOPK):
        within = pl.multiple_of(lax.rem(picks[t], local_blocks) * BLK, BLK)
        places.append((shard - picks[t] // local_blocks, within))
        if t:
            dead = picks[t] == picks[0]
            for u in range(1, t):
                dead = jnp.logical_or(dead, picks[t] == picks[u])
            live.append(jnp.logical_not(dead))
    seed_base = seed_ref[head] + own_block * BLK * 40503

    q = q_ref[...]
    do = do_ref[...]
    q_t = q.T
    do_t = do.T
    chunks = [(t, c, (c * SUB if t == 0 else 0)) for t in range(TOPK) for c in range(BLK // SUB)]
    corner = (lax.broadcasted_iota(jnp.int32, (SUB, SUB), 0)
              <= lax.broadcasted_iota(jnp.int32, (SUB, SUB), 1))

    peaks = None
    for t in range(TOPK):
        slot, within = places[t]
        tops = []
        for c in range(BLK // SUB):
            lo = c * SUB if t == 0 else 0
            keys = kv_ref[slot, 0, pl.ds(within + c * SUB, SUB), :]
            s = dot(keys, q_t[:, lo:])
            if t == 0:
                edge = jnp.where(corner, s[:, :SUB], -jnp.inf)
                s = edge if lo + SUB == BLK else jnp.concatenate([edge, s[:, SUB:]], axis=1)
            s_ref[t, c * SUB:(c + 1) * SUB, lo:] = s
            top = jnp.max(s, axis=0, keepdims=True)
            if lo:
                top = jnp.concatenate([jnp.full((1, lo), -jnp.inf, jnp.float32), top], axis=1)
            tops.append(top)
        top = jnp.maximum(jnp.maximum(tops[0], tops[1]), jnp.maximum(tops[2], tops[3]))
        if t:
            top = jnp.where(live[t], top, -jnp.inf)
        peaks = top if peaks is None else jnp.maximum(peaks, top)
    peak = peaks * exp_scale

    total = jnp.zeros((1, BLK), jnp.float32)
    delta = jnp.zeros((1, BLK), jnp.float32)
    for t, c, lo in chunks:
        slot, within = places[t]
        rows = slice(c * SUB, (c + 1) * SUB)
        values = kv_ref[slot, 1, pl.ds(within + c * SUB, SUB), :]
        pg = dot(values, do_t[:, lo:])
        base = peak if t == 0 else jnp.where(live[t], peak, 3e38)
        e = jnp.exp2(s_ref[t, rows, lo:] * exp_scale - base[:, lo:])
        keep = kept(hash_ref[rows, lo:] + (seed_base + picks[t] * BLK * 9973))
        d = jnp.where(keep, e, 0.0)
        pg = jnp.where(keep, pg, 0.0)
        s_ref[t, rows, lo:] = e
        pg_ref[t, rows, lo:] = pg
        d_ref[t, rows, lo:] = d.astype(jnp.bfloat16)
        e_sum = jnp.sum(e, axis=0, keepdims=True)
        dp_sum = jnp.sum(e * pg, axis=0, keepdims=True)
        if lo:
            pad = jnp.zeros((1, lo), jnp.float32)
            e_sum = jnp.concatenate([pad, e_sum], axis=1)
            dp_sum = jnp.concatenate([pad, dp_sum], axis=1)
        total = total + e_sum
        delta = delta + dp_sum

    inv = 1.0 / total
    delta = delta * inv
    q_n = (q_t.astype(jnp.float32) * inv).astype(jnp.bfloat16).T
    do_n = (do_t.astype(jnp.float32) * inv).astype(jnp.bfloat16).T
    qg_t = jnp.zeros((HD, BLK), jnp.float32)
    for t in range(TOPK):
        slot, within = places[t]
        for c in range(BLK // SUB):
            lo = c * SUB if t == 0 else 0
            rows = slice(c * SUB, (c + 1) * SUB)
            sg = s_ref[t, rows, lo:] * (pg_ref[t, rows, lo:] - delta[:, lo:])
            sg_ref[t, rows, lo:] = sg.astype(jnp.bfloat16)
        acc_ref[slot, 1, pl.ds(within, BLK), :] += dot(d_ref[t], do_n)
        acc_ref[slot, 0, pl.ds(within, BLK), :] += dot(sg_ref[t], q_n)
        qg_t = qg_t + dot(kt_ref[slot, :, pl.ds(within, BLK)], sg_ref[t])
    qg_ref[...] = (qg_t * (inv * (keep_gain * factor))).T

    @pl.when(step == steps - 1)
    def _():
        for part, scale in ((0, keep_gain * factor), (1, keep_gain)):
            own_ref[part] = acc_ref[0, part] * scale
            for slot in range(1, window):
                far_ref[slot - 1, part] = (acc_ref[slot, part] * scale).astype(jnp.bfloat16)


def block_grads(query, out_grad, stacked, chosen, drop_seed, shard):
    rows = query.shape[0]
    local_heads = query.shape[1] // HD
    local_blocks = rows // BLK
    window = stacked.shape[0]
    steps = local_heads * local_blocks
    tile = pl.BlockSpec((BLK, HD), lambda i, *_: (lax.rem(i, local_blocks), i // local_blocks))
    flops = steps * TOPK * 5 * 2 * BLK * BLK * HD
    kernel = lambda *refs: grads_kernel(local_blocks, window, steps, *refs)
    return pl.pallas_call(
        kernel,
        name="block_grads",
        grid_spec=pltpu.PrefetchScalarGridSpec(
            num_scalar_prefetch=3,
            grid=(steps,),
            in_specs=[tile, tile, pl.BlockSpec((window, 2, rows, HD), lambda i, *_: (0, 0, 0, 0))],
            out_specs=[
                tile,
                pl.BlockSpec((window - 1, 2, rows, HD), lambda i, *_: (0, 0, 0, 0)),
                pl.BlockSpec((2, rows, HD), lambda i, *_: (0, 0, 0)),
            ],
            scratch_shapes=[
                pltpu.VMEM((TOPK, BLK, BLK), jnp.float32),
                pltpu.VMEM((TOPK, BLK, BLK), jnp.float32),
                pltpu.VMEM((TOPK, BLK, BLK), jnp.bfloat16),
                pltpu.VMEM((TOPK, BLK, BLK), jnp.bfloat16),
                pltpu.VMEM((window, 2, rows, HD), jnp.float32),
                pltpu.VMEM((window, HD, rows), jnp.bfloat16),
                pltpu.VMEM((BLK, BLK), jnp.int32),
            ],
        ),
        out_shape=[
            jax.ShapeDtypeStruct((rows, local_heads * HD), jnp.float32),
            jax.ShapeDtypeStruct((window - 1, 2, rows, HD), jnp.bfloat16),
            jax.ShapeDtypeStruct((2, rows, HD), jnp.float32),
        ],
        compiler_params=pltpu.CompilerParams(vmem_limit_bytes=60 << 20),
        cost_estimate=pl.CostEstimate(flops=flops, bytes_accessed=20 << 20, transcendentals=steps * TOPK * BLK * BLK),
    )(chosen.reshape(-1), drop_seed, shard.reshape(1), query, out_grad, stacked)


def local(query, key, value, out_grad, chosen, drop_seed):
    rows = query.shape[0]
    local_heads = query.shape[1] // HD
    window = min(SPAN, lax.axis_size("seq") // 2)
    shard = lax.axis_index("seq").astype(jnp.int32)
    head_rank = lax.axis_index("head")
    kv_col = head_rank * local_heads // (HEADS // KVH) * HD
    own_pair = jnp.stack(
        [
            lax.dynamic_slice_in_dim(key, kv_col, HD, 1),
            lax.dynamic_slice_in_dim(value, kv_col, HD, 1),
        ]
    )
    stacked = jnp.stack([own_pair] + [shifted(own_pair, "seq", d) for d in range(1, window)])
    query_grad, far, carried = block_grads(query, out_grad, stacked, chosen, drop_seed, shard)
    for d in range(1, window):
        carried = carried + shifted(far[d - 1], "seq", -d).astype(jnp.float32)
    ranks = lax.axis_size("head")
    pieces = carried.reshape(2, ranks, rows // ranks, HD)
    swapped = lax.all_to_all(pieces, "head", 1, 1, tiled=True)
    summed = swapped.reshape(2, KVH, ranks // KVH, rows // ranks, HD).sum(2)
    both = summed.transpose(0, 2, 1, 3).reshape(2, rows // ranks, KVH * HD)
    return (query_grad, both[0], both[1])


def solution(mesh):
    in_specs = (
        P("seq", "head"),
        P("seq", None),
        P("seq", None),
        P("seq", "head"),
        P("head", "seq", None),
        P("head"),
    )
    out_specs = (P("seq", "head"), P(("seq", "head"), None), P(("seq", "head"), None))
    return jax.shard_map(local, mesh=mesh, in_specs=in_specs, out_specs=out_specs, check_vma=False)
```

time: 917 us -> 213 us (0.23); the launches traced: 908 us -> 213 us
  loops' own time: 252 us -> 0 us
  other arithmetic: 228 us -> 1.87 us
  matrix products: 175 us -> 0 us
  waiting for transfers between devices: 168 us -> 72.4 us
  Pallas kernels: 0 us -> 90.6 us
  local copies, waits for them, and re-layouts: 53.8 us -> 5.8 us
  blocking collectives: 0 us -> 17 us
  between operations: 14.2 us -> 0.77 us
    another operation x1 -> x0, loops' own time: 252 us -> none  [local(): lax.fori_loop(0, local_heads * local_blocks, visit, (start_grad, start_pa...]
    dot_general x96 -> x0, matrix products: 175 us -> none  [the longest x16 66 us: block_grads(): pgrad = jnp.dot(out_block, value_sel.T, preferred_element_type=jnp.float32)]
    dynamic_update_slice x65 -> x0, other arithmetic: 125 us -> none  [the longest x64 124 us: visit(): lax.dynamic_update_slice(partial_value, current + update, (slot_index, 0,...]
    pallas_call x0 -> x1, Pallas kernels: none -> 90.6 us  [block_grads(): pl.pallas_call(kernel, name='block_grads', grid_spec=pltpu.PrefetchScalar...]
    reduce_scatter x2 -> x0, waiting for transfers between devices: 66.9 us -> none  [the longest x1 34.3 us: local(): lax.psum_scatter(widened[1], 'head', scatter_dimension=0, tiled=True)]
    reduce_or x32 -> x0, other arithmetic: 39.8 us -> none  [visit(): jnp.any(picks[:entry] == target)]
    convert_element_type x16 -> x0, other arithmetic: 35.7 us -> none  [block_grads(): dropped = (probs * gains).astype(jnp.bfloat16)]
    ppermute x6, waiting for transfers between devices: 101 us -> 72.4 us  [shifted(): return lax.ppermute(array, axis, pairs)]
  transfers between devices with their start and end apart: 8 -> 6, of which waited for: 8 -> 4; matrix products, arithmetic and copies ran while one was open for 0% -> 0% of each run, Pallas kernels for 0% -> 0%
where the time goes in v1:
time: 213 us
  Pallas kernels  90.6 us (43%)
  waiting for transfers between devices  72.4 us (34%)
  starting transfers between devices  24.5 us (12%)
  blocking collectives  17 us (8%)
  local copies, waits for them, and re-layouts  5.8 us (3%)
    pallas_call x1, Pallas kernels, block_grads(): pl.pallas_call(kernel, name='block_grads', grid_spec=pltpu.PrefetchScalar...  90.6 us
    ppermute x6, waiting for transfers between devices, shifted(): return lax.ppermute(array, axis, pairs)  72.4 us
    ppermute x6, starting transfers between devices, shifted(): return lax.ppermute(array, axis, pairs)  24.5 us
    all_to_all x1, blocking collectives, local(): swapped = lax.all_to_all(pieces, 'head', 1, 1, tiled=True)  17 us
  transfers between devices with their start and end apart: 6, of which 4 were waited for; matrix products, arithmetic and copies ran while one was open for 0% of the time, Pallas kernels for 0%

profile of v1, /device:TPU:8, one launch (start us, length us, event | category | flops | bytes accessed | tf_op | source)
XLA Modules:
  0.0 213.0 jit_solution(18187352588169546012)
XLA Ops:
  0.7 1.1 dynamic-slice_bitcast_fusion
  1.7 0.1 fusion
  1.8 3.5 %collective-permute-start.1 = (bf16[2,1024,128]{2,1,0:T(8,128)(2,1)S(1)}, bf16[2,1024,128]{2,1,0:T(8,128)(2,1)S(1)}, u32[]{:S(2)}, u32[]{:S(2)}) collective-permute-start(bf16[2,1024,128]{2,1,0:T(8,128)(2,1)S(1)} %get-tuple-element.18), channel_id=1, source_target_pairs={{0,8},{4,12},{8,16},{12,20},{16,24},{20,28},{1,9},{5,13},{9,17},{1... | collective-permute-start | bytes 1572872 | tf_op jit(solution)/shard_map/ppermute | solution.py:27
  5.3 3.4 %collective-permute-start = (bf16[2,1024,128]{2,1,0:T(8,128)(2,1)S(1)}, bf16[2,1024,128]{2,1,0:T(8,128)(2,1)S(1)}, u32[]{:S(2)}, u32[]{:S(2)}) collective-permute-start(bf16[2,1024,128]{2,1,0:T(8,128)(2,1)S(1)} %get-tuple-element.18), channel_id=1, source_target_pairs={{0,4},{4,8},{8,12},{12,16},{16,20},{20,24},{24,28},{1,5},{5,9},{9,... | collective-permute-start | bytes 1572872 | tf_op jit(solution)/shard_map/ppermute | solution.py:27
  8.7 3.0 %collective-permute-start.2 = (bf16[2,1024,128]{2,1,0:T(8,128)(2,1)S(1)}, bf16[2,1024,128]{2,1,0:T(8,128)(2,1)S(1)}, u32[]{:S(2)}, u32[]{:S(2)}) collective-permute-start(bf16[2,1024,128]{2,1,0:T(8,128)(2,1)S(1)} %get-tuple-element.18), channel_id=1, source_target_pairs={{0,12},{4,16},{8,20},{12,24},{16,28},{1,13},{5,17},{9,21},{13,25},... | collective-permute-start | bytes 1572872 | tf_op jit(solution)/shard_map/ppermute | solution.py:27
  11.7 0.1 copy.17
  11.8 0.6 reshape.23.refs_0_
  12.4 6.1 %collective-permute-done.1 = bf16[2,1024,128]{2,1,0:T(8,128)(2,1)S(1)} collective-permute-done((bf16[2,1024,128]{2,1,0:T(8,128)(2,1)S(1)}, bf16[2,1024,128]{2,1,0:T(8,128)(2,1)S(1)}, u32[]{:S(2)}, u32[]{:S(2)}) %collective-permute-start.1) | collective-permute-done | bytes 524320 | tf_op jit(solution)/shard_map/ppermute | solution.py:27
  18.5 12.3 %collective-permute-done = bf16[2,1024,128]{2,1,0:T(8,128)(2,1)S(1)} collective-permute-done((bf16[2,1024,128]{2,1,0:T(8,128)(2,1)S(1)}, bf16[2,1024,128]{2,1,0:T(8,128)(2,1)S(1)}, u32[]{:S(2)}, u32[]{:S(2)}) %collective-permute-start) | collective-permute-done | bytes 524320 | tf_op jit(solution)/shard_map/ppermute | solution.py:27
  30.8 1.6 pad_maximum_fusion.refs_5_
  32.4 90.6 %block_grads.1 = (f32[1024,1024]{1,0:T(8,128)}, bf16[3,2,1024,128]{3,2,1,0:T(8,128)(2,1)}, f32[2,1024,128]{2,1,0:T(8,128)}) custom-call(s32[64]{0:T(128)} %reshape.23.refs_0_, s32[8]{0:T(128)} %refs_1_.1, s32[1]{0:T(128)} %bitcast.refs_2_, bf16[1024,1024]{1,0:T(8,128)(2,1)} %refs_3_.1, bf16[1024,1024]{1,0:T(8,128)(2,1)} %refs_4_.1, ...), custom_call_target="tpu_custom_call" | custom-call | flops 21474836480 | bytes 20971520 | tf_op jit(solution)/shard_map/block_grads/pallas_call | solution.py:160
  123.1 1.5 slice_bitcast_fusion.2
  124.6 11.4 %collective-permute-start.3 = (bf16[2,1024,128]{2,1,0:T(8,128)(2,1)S(1)}, bf16[2,1024,128]{2,1,0:T(8,128)(2,1)S(1)}, u32[]{:S(2)}, u32[]{:S(2)}) collective-permute-start(bf16[2,1024,128]{2,1,0:T(8,128)(2,1)S(1)} %get-tuple-element.12), channel_id=1, source_target_pairs={{4,0},{8,4},{12,8},{16,12},{20,16},{24,20},{28,24},{5,1},{9,5},{13... | collective-permute-start | bytes 1572872 | tf_op jit(solution)/shard_map/ppermute | solution.py:27
  136.1 1.3 collective-permute-start.5
  137.4 1.9 collective-permute-start.4
  139.3 23.5 %collective-permute-done.3 = bf16[2,1024,128]{2,1,0:T(8,128)(2,1)S(1)} collective-permute-done((bf16[2,1024,128]{2,1,0:T(8,128)(2,1)S(1)}, bf16[2,1024,128]{2,1,0:T(8,128)(2,1)S(1)}, u32[]{:S(2)}, u32[]{:S(2)}) %collective-permute-start.3) | collective-permute-done | bytes 524320 | tf_op jit(solution)/shard_map/ppermute | solution.py:27
  162.8 30.6 %collective-permute-done.4 = bf16[2,1024,128]{2,1,0:T(8,128)(2,1)S(1)} collective-permute-done((bf16[2,1024,128]{2,1,0:T(8,128)(2,1)S(1)}, bf16[2,1024,128]{2,1,0:T(8,128)(2,1)S(1)}, u32[]{:S(2)}, u32[]{:S(2)}) %collective-permute-start.4) | collective-permute-done | bytes 524320 | tf_op jit(solution)/shard_map/ppermute | solution.py:27
  193.3 0.2 convert_add_fusion
  193.5 0.1 copy.18
  193.6 17.0 %all_to_all.5 = f32[2,4,256,128]{3,2,0,1:T(8,128)S(1)} all-to-all(f32[2,4,256,128]{3,2,0,1:T(8,128)S(1)} %copy.18), channel_id=1, replica_groups=mesh['seq'=8,'head'=4] {'head'}, dimensions={1} | all-to-all | bytes 2097152 | tf_op jit(solution)/shard_map/all_to_all | solution.py:211
  210.6 0.3 copy.19
  211.0 0.1 fusion.1
  211.0 1.0 copy.21
  212.0 1.0 copy.20
  (6 shorter events, 0.0 us)
Async XLA Ops:
  0.6 11.1 %copy-start.1 = (s32[8,2,4]{0,2,1:T(4,128)S(1)}, s32[8,2,4]{0,2,1:T(4,128)}, u32[]{:S(2)}) copy-start(s32[8,2,4]{0,2,1:T(4,128)} %param.10) | copy-start | bytes 772
  1.8 16.7 %collective-permute-start.1 = (bf16[2,1024,128]{2,1,0:T(8,128)(2,1)S(1)}, bf16[2,1024,128]{2,1,0:T(8,128)(2,1)S(1)}, u32[]{:S(2)}, u32[]{:S(2)}) collective-permute-start(bf16[2,1024,128]{2,1,0:T(8,128)(2,1)S(1)} %get-tuple-element.18), channel_id=1, source_target_pairs={{0,8},{4,12},{8,16},{12,20},{16,24},{20,28},{1,9},{5,13},{9,17},{1... | collective-permute-start | bytes 1572872 | tf_op jit(solution)/shard_map/ppermute | solution.py:27
  5.3 25.5 %collective-permute-start = (bf16[2,1024,128]{2,1,0:T(8,128)(2,1)S(1)}, bf16[2,1024,128]{2,1,0:T(8,128)(2,1)S(1)}, u32[]{:S(2)}, u32[]{:S(2)}) collective-permute-start(bf16[2,1024,128]{2,1,0:T(8,128)(2,1)S(1)} %get-tuple-element.18), channel_id=1, source_target_pairs={{0,4},{4,8},{8,12},{12,16},{16,20},{20,24},{24,28},{1,5},{5,9},{9,... | collective-permute-start | bytes 1572872 | tf_op jit(solution)/shard_map/ppermute | solution.py:27
  8.7 22.1 %collective-permute-start.2 = (bf16[2,1024,128]{2,1,0:T(8,128)(2,1)S(1)}, bf16[2,1024,128]{2,1,0:T(8,128)(2,1)S(1)}, u32[]{:S(2)}, u32[]{:S(2)}) collective-permute-start(bf16[2,1024,128]{2,1,0:T(8,128)(2,1)S(1)} %get-tuple-element.18), channel_id=1, source_target_pairs={{0,12},{4,16},{8,20},{12,24},{16,28},{1,13},{5,17},{9,21},{13,25},... | collective-permute-start | bytes 1572872 | tf_op jit(solution)/shard_map/ppermute | solution.py:27
  123.1 70.2 %copy-start = (f32[2,1024,128]{2,1,0:T(8,128)S(1)}, f32[2,1024,128]{2,1,0:T(8,128)}, u32[]{:S(2)}) copy-start(f32[2,1024,128]{2,1,0:T(8,128)} %get-tuple-element.7) | copy-start | bytes 3145732
  124.6 38.1 %collective-permute-start.3 = (bf16[2,1024,128]{2,1,0:T(8,128)(2,1)S(1)}, bf16[2,1024,128]{2,1,0:T(8,128)(2,1)S(1)}, u32[]{:S(2)}, u32[]{:S(2)}) collective-permute-start(bf16[2,1024,128]{2,1,0:T(8,128)(2,1)S(1)} %get-tuple-element.12), channel_id=1, source_target_pairs={{4,0},{8,4},{12,8},{16,12},{20,16},{24,20},{28,24},{5,1},{9,5},{13... | collective-permute-start | bytes 1572872 | tf_op jit(solution)/shard_map/ppermute | solution.py:27
  136.1 26.7 %collective-permute-start.5 = (bf16[2,1024,128]{2,1,0:T(8,128)(2,1)S(1)}, bf16[2,1024,128]{2,1,0:T(8,128)(2,1)S(1)}, u32[]{:S(2)}, u32[]{:S(2)}) collective-permute-start(bf16[2,1024,128]{2,1,0:T(8,128)(2,1)S(1)} %get-tuple-element.13), channel_id=1, source_target_pairs={{12,0},{16,4},{20,8},{24,12},{28,16},{13,1},{17,5},{21,9},{25,13},... | collective-permute-start | bytes 1572872 | tf_op jit(solution)/shard_map/ppermute | solution.py:27
  137.4 55.9 %collective-permute-start.4 = (bf16[2,1024,128]{2,1,0:T(8,128)(2,1)S(1)}, bf16[2,1024,128]{2,1,0:T(8,128)(2,1)S(1)}, u32[]{:S(2)}, u32[]{:S(2)}) collective-permute-start(bf16[2,1024,128]{2,1,0:T(8,128)(2,1)S(1)} %get-tuple-element.14), channel_id=1, source_target_pairs={{8,0},{12,4},{16,8},{20,12},{24,16},{28,20},{9,1},{13,5},{17,9},{2... | collective-permute-start | bytes 1572872 | tf_op jit(solution)/shard_map/ppermute | solution.py:27

commit v2 on v1

--- a/solution.py
+++ b/solution.py
@@ -38,15 +38,26 @@
     return jnp.dot(a, b, preferred_element_type=jnp.float32)
 
 
-def grads_kernel(local_blocks, window, steps, chosen_ref, seed_ref, shard_ref, q_ref, do_ref, kv_ref,
-                 qg_ref, far_ref, own_ref, s_ref, pg_ref, d_ref, sg_ref, acc_ref, kt_ref, hash_ref):
+def grads_kernel(local_blocks, window, steps, chosen_ref, seed_ref, place_ref, q_ref, do_ref, key_ref, value_ref,
+                 gathered_ref, qg_ref, far_ref, own_ref, s_ref, pg_ref, d_ref, sg_ref, acc_ref, kt_ref, hash_ref, kv_ref,
+                 load_sem):
     step = pl.program_id(0)
 
     @pl.when(step == 0)
     def _():
+        col = pl.ds(pl.multiple_of(place_ref[1], HD), HD)
+        loads = [
+            pltpu.make_async_copy(key_ref.at[:, col], kv_ref.at[0, 0], load_sem.at[0]),
+            pltpu.make_async_copy(value_ref.at[:, col], kv_ref.at[0, 1], load_sem.at[1]),
+            pltpu.make_async_copy(gathered_ref, kv_ref.at[pl.ds(1, window - 1)], load_sem.at[2]),
+        ]
+        for load in loads:
+            load.start()
         acc_ref[...] = jnp.zeros_like(acc_ref)
         d_ref[0] = jnp.zeros((BLK, BLK), jnp.bfloat16)
         sg_ref[0] = jnp.zeros((BLK, BLK), jnp.bfloat16)
+        for load in loads:
+            load.wait()
         for slot in range(window):
             kt_ref[slot] = kv_ref[slot, 0].T
         hash_ref[...] = (lax.broadcasted_iota(jnp.int32, (BLK, BLK), 0) * 9973
@@ -54,7 +65,7 @@
 
     head = step // local_blocks
     block = lax.rem(step, local_blocks)
-    shard = shard_ref[0]
+    shard = place_ref[0]
     own_block = shard * local_blocks + block
     picks = [chosen_ref[step * TOPK + t] for t in range(TOPK)]
     places = []
@@ -148,11 +159,11 @@
                 far_ref[slot - 1, part] = (acc_ref[slot, part] * scale).astype(jnp.bfloat16)
 
 
-def block_grads(query, out_grad, stacked, chosen, drop_seed, shard):
+def block_grads(query, out_grad, key, value, gathered, chosen, drop_seed, place):
     rows = query.shape[0]
     local_heads = query.shape[1] // HD
     local_blocks = rows // BLK
-    window = stacked.shape[0]
+    window = gathered.shape[0] + 1
     steps = local_heads * local_blocks
     tile = pl.BlockSpec((BLK, HD), lambda i, *_: (lax.rem(i, local_blocks), i // local_blocks))
     flops = steps * TOPK * 5 * 2 * BLK * BLK * HD
@@ -163,7 +174,7 @@
         grid_spec=pltpu.PrefetchScalarGridSpec(
             num_scalar_prefetch=3,
             grid=(steps,),
-            in_specs=[tile, tile, pl.BlockSpec((window, 2, rows, HD), lambda i, *_: (0, 0, 0, 0))],
+            in_specs=[tile, tile] + [pl.BlockSpec(memory_space=pl.ANY)] * 3,
             out_specs=[
                 tile,
                 pl.BlockSpec((window - 1, 2, rows, HD), lambda i, *_: (0, 0, 0, 0)),
@@ -177,6 +188,8 @@
                 pltpu.VMEM((window, 2, rows, HD), jnp.float32),
                 pltpu.VMEM((window, HD, rows), jnp.bfloat16),
                 pltpu.VMEM((BLK, BLK), jnp.int32),
+                pltpu.VMEM((window, 2, rows, HD), jnp.bfloat16),
+                pltpu.SemaphoreType.DMA((3,)),
             ],
         ),
         out_shape=[
@@ -186,28 +199,270 @@
         ],
         compiler_params=pltpu.CompilerParams(vmem_limit_bytes=60 << 20),
         cost_estimate=pl.CostEstimate(flops=flops, bytes_accessed=20 << 20, transcendentals=steps * TOPK * BLK * BLK),
-    )(chosen.reshape(-1), drop_seed, shard.reshape(1), query, out_grad, stacked)
+    )(chosen.reshape(-1), drop_seed, place, query, out_grad, key, value, gathered)
+
+
+CHUNKS = 4
+
+
+def seq_peer(by):
+    size = lax.axis_size("seq")
+    return {"seq": lax.rem(lax.axis_index("seq") + by + size, size)}
+
+
+def meet(peers):
+    barrier = pltpu.get_barrier_semaphore()
+    for peer in peers:
+        pl.semaphore_signal(barrier, inc=1, device_id=peer, device_id_type=pl.DeviceIdType.MESH)
+    pl.semaphore_wait(barrier, len(peers))
+
+
+def remote(src, dst, send, recv, peer):
+    return pltpu.make_async_remote_copy(
+        src_ref=src, dst_ref=dst, send_sem=send, recv_sem=recv, device_id=peer,
+        device_id_type=pl.DeviceIdType.MESH,
+    )
+
+
+def gather_kernel(key_ref, value_ref, far_ref, send_sem, recv_sem):
+    shard = lax.axis_index("seq")
+    odd = lax.rem(shard, 2)
+    col = pl.ds(pl.multiple_of(lax.axis_index("head") * HD, HD), HD)
+    half = key_ref.shape[0] // 2
+    mate = {"seq": shard + 1 - 2 * odd}
+    ahead = seq_peer(2)
+    meet([ahead, seq_peer(-2), mate])
+
+    def own(c):
+        return (key_ref, value_ref)[c // 2].at[pl.ds(c % 2 * half, half), col]
+
+    def far(k, c):
+        return far_ref.at[k, c // 2, pl.ds(c % 2 * half, half), :]
+
+    def own_ahead(c):
+        return remote(own(c), far(1, c), send_sem.at[0, c], recv_sem.at[1, c], ahead)
+
+    def own_mate(c):
+        return remote(own(c), far(0, c), send_sem.at[1, c], recv_sem.at[0, c], mate)
+
+    def pass_mate(c, k):
+        return remote(far(1, c), far(k, c), send_sem.at[2, c], recv_sem.at[k, c], mate)
+
+    def pass_ahead(c):
+        return remote(far(0, c), far(2, c), send_sem.at[3, c], recv_sem.at[2, c], ahead)
+
+    for c in range(CHUNKS):
+        own_ahead(c).start()
+
+        @pl.when(odd == 0)
+        def _():
+            own_mate(c).start()
+
+    for c in range(CHUNKS):
+        own_ahead(c).wait_recv()
+
+        @pl.when(odd == 0)
+        def _():
+            pass_mate(c, 2).start()
+
+        @pl.when(odd == 1)
+        def _():
+            pass_mate(c, 0).start()
+
+        if c:
+            @pl.when(odd == 0)
+            def _():
+                own_mate(c - 1).wait_recv()
+                pass_ahead(c - 1).start()
+
+    @pl.when(odd == 0)
+    def _():
+        own_mate(CHUNKS - 1).wait_recv()
+        pass_ahead(CHUNKS - 1).start()
+        for c in range(CHUNKS):
+            pass_ahead(c).wait_recv()
+            own_mate(c).wait_send()
+            pass_mate(c, 2).wait_send()
+            pass_ahead(c).wait_send()
+
+    @pl.when(odd == 1)
+    def _():
+        for c in range(CHUNKS):
+            own_mate(c).wait_recv()
+            pass_ahead(c).wait_recv()
+            pass_mate(c, 0).wait_send()
+
+    for c in range(CHUNKS):
+        own_ahead(c).wait_send()
+
+
+def gather(key, value):
+    rows = key.shape[0]
+    return pl.pallas_call(
+        gather_kernel,
+        name="gather",
+        out_shape=jax.ShapeDtypeStruct((3, 2, rows, HD), jnp.bfloat16),
+        in_specs=[pl.BlockSpec(memory_space=pl.ANY)] * 2,
+        out_specs=pl.BlockSpec(memory_space=pl.ANY),
+        scratch_shapes=[pltpu.SemaphoreType.DMA((4, CHUNKS)), pltpu.SemaphoreType.DMA((3, CHUNKS))],
+        compiler_params=pltpu.CompilerParams(collective_id=0, has_side_effects=True),
+    )(key, value)
+
+
+def reduce_kernel(ranks, far_ref, own_ref, kg_ref, vg_ref, in_far, in_near, in_two, in_own, up_near, up_two,
+                  in_head, up_head, total, send_sem, recv_sem, head_send, head_recv):
+    shard = lax.axis_index("seq")
+    rank = lax.axis_index("head")
+    odd = lax.rem(shard, 2)
+    mate = {"seq": shard + 1 - 2 * odd}
+    back = seq_peer(-2)
+    others = [{"head": lax.rem(rank + d, ranks)} for d in range(1, ranks)]
+    meet([back, seq_peer(2), mate] + others)
+    piece = in_near.shape[2]
+
+    def rows(c):
+        return pl.ds(c * piece, piece)
+
+    def far_back(c):
+        return remote(far_ref.at[2, :, rows(c)], in_far.at[c], send_sem.at[0, c], recv_sem.at[0, c], back)
+
+    def own_mate(c):
+        return remote(far_ref.at[0, :, rows(c)], in_own.at[c], send_sem.at[0, c], recv_sem.at[1, c], mate)
+
+    def far_mate(c):
+        return remote(far_ref.at[2, :, rows(c)], in_near.at[c], send_sem.at[1, c], recv_sem.at[2, c], mate)
+
+    def near_mate(c):
+        return remote(up_near.at[c], in_near.at[c], send_sem.at[1, c], recv_sem.at[2, c], mate)
+
+    def two_back(c):
+        return remote(up_two.at[c], in_two.at[c], send_sem.at[2, c], recv_sem.at[3, c], back)
+
+    def to_head(c):
+        return remote(up_head.at[c], in_head.at[rank], head_send.at[c], head_recv.at[rank], {"head": c})
+
+    for c in range(ranks):
+        @pl.when(odd == 0)
+        def _():
+            far_back(c).start()
+
+        @pl.when(odd == 1)
+        def _():
+            far_mate(c).start()
+
+    @pl.when(odd == 1)
+    def _():
+        for c in range(ranks):
+            own_mate(c).start()
+
+    def stage_near(c):
+        @pl.when(odd == 0)
+        def _():
+            far_back(c).wait_recv()
+            up_near[c] = (far_ref[0, :, rows(c)].astype(jnp.float32) + in_far[c].astype(jnp.float32)).astype(jnp.bfloat16)
+            near_mate(c).start()
+
+    def stage_two(c):
+        near_mate(c).wait_recv()
+        up_two[c] = (far_ref[1, :, rows(c)].astype(jnp.float32) + in_near[c].astype(jnp.float32)).astype(jnp.bfloat16)
+        two_back(c).start()
+
+    def stage_own(c):
+        two_back(c).wait_recv()
+        total[c] = own_ref[:, rows(c)] + in_two[c].astype(jnp.float32)
+
+        @pl.when(odd == 0)
+        def _():
+            own_mate(c).wait_recv()
+            total[c] += in_own[c].astype(jnp.float32)
+
+        @pl.when(rank == c)
+        def _():
+            kg_ref[:, c * HD:(c + 1) * HD] = total[c, 0]
+            vg_ref[:, c * HD:(c + 1) * HD] = total[c, 1]
+
+        @pl.when(rank != c)
+        def _():
+            up_head[c] = total[c].astype(jnp.bfloat16)
+            to_head(c).start()
+
+    for k in range(ranks + 2):
+        if k < ranks:
+            stage_near(k)
+        if 0 <= k - 1 < ranks:
+            stage_two(k - 1)
+        if 0 <= k - 2:
+            stage_own(k - 2)
+
+    for c in range(ranks):
+        @pl.when(rank != c)
+        def _():
+            remote(up_head.at[c], in_head.at[c], head_send.at[c], head_recv.at[c], {"head": c}).wait_recv()
+            kg_ref[:, c * HD:(c + 1) * HD] = in_head[c, 0].astype(jnp.float32)
+            vg_ref[:, c * HD:(c + 1) * HD] = in_head[c, 1].astype(jnp.float32)
+            to_head(c).wait_send()
+
+        two_back(c).wait_send()
+
+        @pl.when(odd == 0)
+        def _():
+            far_back(c).wait_send()
+            near_mate(c).wait_send()
+
+        @pl.when(odd == 1)
+        def _():
+            own_mate(c).wait_send()
+            far_mate(c).wait_send()
+
+
+def reduce(far, own):
+    ranks = lax.axis_size("head")
+    rows = own.shape[1]
+    piece = rows // ranks
+    part = pltpu.VMEM((ranks, 2, piece, HD), jnp.bfloat16)
+    return pl.pallas_call(
+        lambda *refs: reduce_kernel(ranks, *refs),
+        name="reduce",
+        out_shape=[jax.ShapeDtypeStruct((piece, ranks * HD), jnp.float32)] * 2,
+        in_specs=[pl.BlockSpec(memory_space=pltpu.VMEM)] * 2,
+        out_specs=[pl.BlockSpec(memory_space=pltpu.VMEM)] * 2,
+        scratch_shapes=[part] * 8 + [
+            pltpu.VMEM((ranks, 2, piece, HD), jnp.float32),
+            pltpu.SemaphoreType.DMA((3, ranks)),
+            pltpu.SemaphoreType.DMA((4, ranks)),
+            pltpu.SemaphoreType.DMA((ranks,)),
+            pltpu.SemaphoreType.DMA((ranks,)),
+        ],
+        compiler_params=pltpu.CompilerParams(collective_id=1, has_side_effects=True, vmem_limit_bytes=32 << 20),
+    )(far, own)
 
 
 def local(query, key, value, out_grad, chosen, drop_seed):
     rows = query.shape[0]
     local_heads = query.shape[1] // HD
-    window = min(SPAN, lax.axis_size("seq") // 2)
-    shard = lax.axis_index("seq").astype(jnp.int32)
-    head_rank = lax.axis_index("head")
-    kv_col = head_rank * local_heads // (HEADS // KVH) * HD
-    own_pair = jnp.stack(
-        [
-            lax.dynamic_slice_in_dim(key, kv_col, HD, 1),
-            lax.dynamic_slice_in_dim(value, kv_col, HD, 1),
-        ]
-    )
-    stacked = jnp.stack([own_pair] + [shifted(own_pair, "seq", d) for d in range(1, window)])
-    query_grad, far, carried = block_grads(query, out_grad, stacked, chosen, drop_seed, shard)
+    size = lax.axis_size("seq")
+    ranks = lax.axis_size("head")
+    window = min(SPAN, size // 2)
+    kv_col = lax.axis_index("head") * local_heads // (HEADS // KVH) * HD
+    place = jnp.stack([lax.axis_index("seq"), kv_col]).astype(jnp.int32)
+    paired = window == 4 and ranks == KVH and size % 2 == 0
+    if paired:
+        gathered = gather(key, value)
+    else:
+        own_pair = jnp.stack(
+            [
+                lax.dynamic_slice_in_dim(key, kv_col, HD, 1),
+                lax.dynamic_slice_in_dim(value, kv_col, HD, 1),
+            ]
+        )
+        gathered = jnp.stack([shifted(own_pair, "seq", d) for d in range(1, window)])
+    query_grad, far, own = block_grads(query, out_grad, key, value, gathered, chosen, drop_seed, place)
+    if paired:
+        key_grad, value_grad = reduce(far, own)
+        return (query_grad, key_grad, value_grad)
     for d in range(1, window):
-        carried = carried + shifted(far[d - 1], "seq", -d).astype(jnp.float32)
-    ranks = lax.axis_size("head")
-    pieces = carried.reshape(2, ranks, rows // ranks, HD)
+        own = own + shifted(far[d - 1], "seq", -d).astype(jnp.float32)
+    pieces = own.reshape(2, ranks, rows // ranks, HD)
     swapped = lax.all_to_all(pieces, "head", 1, 1, tiled=True)
     summed = swapped.reshape(2, KVH, ranks // KVH, rows // ranks, HD).sum(2)
     both = summed.transpose(0, 2, 1, 3).reshape(2, rows // ranks, KVH * HD)

time: 213 us -> 157 us (0.74)
  waiting for transfers between devices: 72.4 us -> 0 us
  Pallas kernels: 90.6 us -> 148 us
  starting transfers between devices: 24.5 us -> 0 us
  blocking collectives: 17 us -> 0 us
    ppermute x6 -> x0, waiting for transfers between devices: 72.4 us -> none  [shifted(): return lax.ppermute(array, axis, pairs)]
    pallas_call x0 -> x2, Pallas kernels: none -> 57 us  [the longest x1 29.5 us: reduce(): pl.pallas_call(lambda *refs: reduce_kernel(ranks, *refs), name='reduce',...]
    ppermute x6 -> x0, starting transfers between devices: 24.5 us -> none  [shifted(): return lax.ppermute(array, axis, pairs)]
    all_to_all x1 -> x0, blocking collectives: 17 us -> none  [local(): swapped = lax.all_to_all(pieces, 'head', 1, 1, tiled=True)]
    unnamed x7, local copies, waits for them, and re-layouts: 2.09 us -> 4.99 us
  transfers between devices with their start and end apart: 6 -> 0, of which waited for: 4 -> 0; matrix products, arithmetic and copies ran while one was open for 0% -> 0% of each run, Pallas kernels for 0% -> 0%
where the time goes in v2:
time: 157 us; the launch traced here: 155 us
  Pallas kernels  148 us (94%)
  local copies, waits for them, and re-layouts  5.59 us (4%)
    pallas_call x1, Pallas kernels, block_grads(): pl.pallas_call(kernel, name='block_grads', grid_spec=pltpu.PrefetchScalar...  91.1 us
    pallas_call x1, Pallas kernels, reduce(): pl.pallas_call(lambda *refs: reduce_kernel(ranks, *refs), name='reduce',...  29.5 us
    pallas_call x1, Pallas kernels, gather(): pl.pallas_call(gather_kernel, name='gather', out_shape=jax.ShapeDtypeStru...  27.5 us
    unnamed x7, local copies, waits for them, and re-layouts  4.99 us

profile of v2, /device:TPU:8, one launch (start us, length us, event | category | flops | bytes accessed | tf_op | source)
XLA Modules:
  0.0 155.0 jit_solution(9537788473426179216)
XLA Ops:
  0.6 0.6 pad_add_fusion.refs_2_
  1.2 0.8 copy.10
  2.0 0.6 reshape.9.refs_0_
  2.6 27.5 %gather.1.refs_7_ = bf16[3,2,1024,128]{3,2,1,0:T(8,128)(2,1)} custom-call(bf16[1024,512]{1,0:T(8,128)(2,1)} %refs_5_.1, bf16[1024,512]{1,0:T(8,128)(2,1)} %refs_6_.1), custom_call_target="tpu_custom_call" | custom-call | tf_op jit(solution)/shard_map/gather/pallas_call | solution.py:301
  30.1 91.1 %block_grads.1 = (f32[1024,1024]{1,0:T(8,128)}, bf16[3,2,1024,128]{3,2,1,0:T(8,128)(2,1)}, f32[2,1024,128]{2,1,0:T(8,128)}) custom-call(s32[64]{0:T(128)} %reshape.9.refs_0_, s32[8]{0:T(128)} %refs_1_.1, s32[2]{0:T(128)} %pad_add_fusion.refs_2_, bf16[1024,1024]{1,0:T(8,128)(2,1)} %refs_3_.1, bf16[1024,1024]{1,0:T(8,128)(2,1)} %refs_4_.1, ...), custom_call_target="tpu_custom_call" | custom-call | flops 21474836480 | bytes 20971520 | tf_op jit(solution)/shard_map/block_grads/pallas_call | solution.py:171
  121.3 0.0 copy-start
  121.3 1.4 copy-done
  122.7 0.0 copy-start.1
  122.7 1.2 copy-done.1
  123.9 29.5 %reduce.1 = (f32[256,512]{1,0:T(8,128)S(1)}, f32[256,512]{1,0:T(8,128)S(1)}) custom-call(bf16[3,2,1024,128]{3,2,1,0:T(8,128)(2,1)S(1)} %copy-done, f32[2,1024,128]{2,1,0:T(8,128)S(1)} %copy-done.1), custom_call_target="tpu_custom_call" | custom-call | tf_op jit(solution)/shard_map/reduce/pallas_call | solution.py:423
  153.4 0.8 copy.13
  154.2 0.8 copy.14
Async XLA Ops:
  121.3 1.4 copy-start
  122.7 1.2 copy-start.1

commit v3 on v2

--- a/solution.py
+++ b/solution.py
@@ -111,33 +111,55 @@
     peak = peaks * exp_scale
 
     total = jnp.zeros((1, BLK), jnp.float32)
-    delta = jnp.zeros((1, BLK), jnp.float32)
     for t, c, lo in chunks:
         slot, within = places[t]
         rows = slice(c * SUB, (c + 1) * SUB)
+        base = peak if t == 0 else jnp.where(live[t], peak, 3e38)
         values = kv_ref[slot, 1, pl.ds(within + c * SUB, SUB), :]
-        pg = dot(values, do_t[:, lo:])
-        base = peak if t == 0 else jnp.where(live[t], peak, 3e38)
+        pg_ref[t, rows, lo:] = dot(values, do_t[:, lo:])
         e = jnp.exp2(s_ref[t, rows, lo:] * exp_scale - base[:, lo:])
-        keep = kept(hash_ref[rows, lo:] + (seed_base + picks[t] * BLK * 9973))
-        d = jnp.where(keep, e, 0.0)
-        pg = jnp.where(keep, pg, 0.0)
         s_ref[t, rows, lo:] = e
-        pg_ref[t, rows, lo:] = pg
-        d_ref[t, rows, lo:] = d.astype(jnp.bfloat16)
         e_sum = jnp.sum(e, axis=0, keepdims=True)
-        dp_sum = jnp.sum(e * pg, axis=0, keepdims=True)
         if lo:
-            pad = jnp.zeros((1, lo), jnp.float32)
-            e_sum = jnp.concatenate([pad, e_sum], axis=1)
-            dp_sum = jnp.concatenate([pad, dp_sum], axis=1)
+            e_sum = jnp.concatenate([jnp.zeros((1, lo), jnp.float32), e_sum], axis=1)
         total = total + e_sum
-        delta = delta + dp_sum
 
     inv = 1.0 / total
-    delta = delta * inv
     q_n = (q_t.astype(jnp.float32) * inv).astype(jnp.bfloat16).T
     do_n = (do_t.astype(jnp.float32) * inv).astype(jnp.bfloat16).T
+
+    def place(t):
+        pick = chosen_ref[step * TOPK + t]
+        return pick, shard - pick // local_blocks, pl.multiple_of(lax.rem(pick, local_blocks) * BLK, BLK)
+
+    def value_sum(t):
+        _, slot, within = place(t)
+        acc_ref[slot, 1, pl.ds(within, BLK), :] += dot(d_ref[t], do_n)
+
+    def gate(t, delta, own):
+        base = seed_base + place(t)[0] * BLK * 9973
+        for c in range(BLK // SUB):
+            lo = c * SUB if own else 0
+            rows = slice(c * SUB, (c + 1) * SUB)
+            e = s_ref[t, rows, lo:]
+            keep = kept(hash_ref[rows, lo:] + base)
+            d_ref[t, rows, lo:] = jnp.where(keep, e, 0.0).astype(jnp.bfloat16)
+            pg = jnp.where(keep, pg_ref[t, rows, lo:], 0.0)
+            pg_ref[t, rows, lo:] = pg
+            dp_sum = jnp.sum(e * pg, axis=0, keepdims=True)
+            if lo:
+                dp_sum = jnp.concatenate([jnp.zeros((1, lo), jnp.float32), dp_sum], axis=1)
+            delta = delta + dp_sum
+        return delta
+
+    def gate_step(t, delta):
+        value_sum(t - 1)
+        return gate(t, delta, False)
+
+    delta = gate(0, jnp.zeros((1, BLK), jnp.float32), True)
+    delta = lax.fori_loop(1, TOPK, gate_step, delta)
+    value_sum(TOPK - 1)
+    delta = delta * inv
     qg_t = jnp.zeros((HD, BLK), jnp.float32)
     for t in range(TOPK):
         slot, within = places[t]
@@ -146,7 +168,6 @@
             rows = slice(c * SUB, (c + 1) * SUB)
             sg = s_ref[t, rows, lo:] * (pg_ref[t, rows, lo:] - delta[:, lo:])
             sg_ref[t, rows, lo:] = sg.astype(jnp.bfloat16)
-        acc_ref[slot, 1, pl.ds(within, BLK), :] += dot(d_ref[t], do_n)
         acc_ref[slot, 0, pl.ds(within, BLK), :] += dot(sg_ref[t], q_n)
         qg_t = qg_t + dot(kt_ref[slot, :, pl.ds(within, BLK)], sg_ref[t])
     qg_ref[...] = (qg_t * (inv * (keep_gain * factor))).T

time: 157 us -> 169 us (1.076)
  Pallas kernels: 148 us -> 160 us
    pallas_call x1, Pallas kernels: 91.1 us -> 103 us  [block_grads(): pl.pallas_call(kernel, name='block_grads', grid_spec=pltpu.PrefetchScalar...]
where the time goes in v3:
time: 169 us; the launch traced here: 167 us
  Pallas kernels  160 us (95%)
  local copies, waits for them, and re-layouts  5.59 us (3%)
    pallas_call x1, Pallas kernels, block_grads(): pl.pallas_call(kernel, name='block_grads', grid_spec=pltpu.PrefetchScalar...  103 us
    pallas_call x1, Pallas kernels, reduce(): pl.pallas_call(lambda *refs: reduce_kernel(ranks, *refs), name='reduce',...  29.5 us
    pallas_call x1, Pallas kernels, gather(): pl.pallas_call(gather_kernel, name='gather', out_shape=jax.ShapeDtypeStru...  27.5 us
    unnamed x7, local copies, waits for them, and re-layouts  4.99 us

profile of v3, /device:TPU:8, one launch (start us, length us, event | category | flops | bytes accessed | tf_op | source)
XLA Modules:
  0.0 166.7 jit_solution(15310882556952821109)
XLA Ops:
  0.6 0.6 pad_add_fusion.refs_2_
  1.2 0.8 copy.10
  2.0 0.6 reshape.9.refs_0_
  2.6 27.5 %gather.1.refs_7_ = bf16[3,2,1024,128]{3,2,1,0:T(8,128)(2,1)} custom-call(bf16[1024,512]{1,0:T(8,128)(2,1)} %refs_5_.1, bf16[1024,512]{1,0:T(8,128)(2,1)} %refs_6_.1), custom_call_target="tpu_custom_call" | custom-call | tf_op jit(solution)/shard_map/gather/pallas_call | solution.py:322
  30.1 102.8 %block_grads.1 = (f32[1024,1024]{1,0:T(8,128)}, bf16[3,2,1024,128]{3,2,1,0:T(8,128)(2,1)}, f32[2,1024,128]{2,1,0:T(8,128)}) custom-call(s32[64]{0:T(128)} %reshape.9.refs_0_, s32[8]{0:T(128)} %refs_1_.1, s32[2]{0:T(128)} %pad_add_fusion.refs_2_, bf16[1024,1024]{1,0:T(8,128)(2,1)} %refs_3_.1, bf16[1024,1024]{1,0:T(8,128)(2,1)} %refs_4_.1, ...), custom_call_target="tpu_custom_call" | custom-call | flops 21474836480 | bytes 20971520 | tf_op jit(solution)/shard_map/block_grads/pallas_call | solution.py:192
  132.9 0.0 copy-start
  132.9 1.4 copy-done
  134.3 0.0 copy-start.1
  134.3 1.2 copy-done.1
  135.6 29.5 %reduce.1 = (f32[256,512]{1,0:T(8,128)S(1)}, f32[256,512]{1,0:T(8,128)S(1)}) custom-call(bf16[3,2,1024,128]{3,2,1,0:T(8,128)(2,1)S(1)} %copy-done, f32[2,1024,128]{2,1,0:T(8,128)S(1)} %copy-done.1), custom_call_target="tpu_custom_call" | custom-call | tf_op jit(solution)/shard_map/reduce/pallas_call | solution.py:444
  165.1 0.8 copy.13
  165.9 0.8 copy.14
Async XLA Ops:
  132.9 1.4 copy-start
  134.3 1.2 copy-start.1
